TPU v7x, 32 devices: a whole 2x2x4 slice. The times are simulated.
32 devices in a mesh: layer: 8 (over y, x, core), tile: 4 (over z).
Axes of the slice: x: 2, y: 2, z: 4, core: 2. Of those that a mesh axis runs over, the one named last changes fastest.
Arguments:
- incident: bfloat16 [4096, 128], P('tile'), may hold values from -6 to 6
- interface: bfloat16 [16, 4096, 4096], P('layer', 'tile'), may hold values from -0.09375 to 0.09375
- eigvec: bfloat16 [16, 4096, 4096], P('layer', 'tile'), may hold values from -0.09375 to 0.09375
- angle: float32 [16, 4096], P('layer'), may hold values from -3.140625 to 3.140625
- decay: float32 [16, 4096], P('layer'), may hold values from 0.002 to 0.15
Outputs:
- fields: bfloat16 [16, 4096, 512], P('layer', 'tile')
- leaving: float32 [16, 4096, 128], P('layer', 'tile')
All inputs are finite; a program needn't handle non-finite values.
Results may differ from a plain program's by a relative error of at most 0.035.
Values sent between devices are 32-bit elements; how exact they have to be, the bound alone decides.
A program may use at most 128 MiB of HBM per device.

v0:
```python
import jax
import jax.numpy as jnp
from jax import lax
from jax.sharding import PartitionSpec as P

DEPTHS = 4


def shifted(x, axis, by):
    peers = lax.axis_size(axis)
    pairs = [(i, i + by) for i in range(peers) if 0 <= i + by < peers]
    return lax.ppermute(x, axis, pairs)


def rotate(block, angle_row, decay_row, frac):
    half = block.shape[1] // 2
    real_part = block[:, :half]
    imag_part = block[:, half:]
    scale = jnp.exp(-frac * decay_row)
    cosine = (scale * jnp.cos(frac * angle_row))[:, None]
    sine = (scale * jnp.sin(frac * angle_row))[:, None]
    return jnp.concatenate(
        [cosine * real_part - sine * imag_part, sine * real_part + cosine * imag_part], axis=1
    )


def advance(current, interface, angle, decay):
    fulls = []
    leaves = []
    for layer_num in range(interface.shape[0]):
        full = lax.all_gather(current, "tile", axis=0, tiled=True)
        fulls.append(full)
        phased = rotate(full, angle[layer_num], decay[layer_num], 1.0).astype(jnp.bfloat16)
        current = jnp.dot(interface[layer_num], phased, preferred_element_type=jnp.float32)
        leaves.append(current)
    return (jnp.stack(fulls), jnp.stack(leaves))


def pick_block(values, block_num, block_width, half):
    real_part = lax.dynamic_slice_in_dim(
        values, block_num * block_width, block_width, values.ndim - 1
    )
    imag_part = lax.dynamic_slice_in_dim(
        values, half + block_num * block_width, block_width, values.ndim - 1
    )
    return jnp.concatenate([real_part, imag_part], axis=values.ndim - 1)


def put_block(values, piece, block_num, block_width, half):
    last = values.ndim - 1
    real_piece = lax.slice_in_dim(piece, 0, block_width, axis=last)
    imag_piece = lax.slice_in_dim(piece, block_width, 2 * block_width, axis=last)
    values = lax.dynamic_update_slice_in_dim(values, real_piece, block_num * block_width, last)
    return lax.dynamic_update_slice_in_dim(values, imag_piece, half + block_num * block_width, last)


def on_device(incident, interface, eigvec, angle, decay):
    groups = lax.axis_size("layer")
    member = lax.axis_index("layer")
    layers_here = interface.shape[0]
    shard_rows = interface.shape[1]
    orders = interface.shape[2]
    width = incident.shape[1]
    half = width // 2
    start_amps = incident.astype(jnp.float32)
    store_full = jnp.zeros((layers_here, orders, width), jnp.float32)
    store_leave = jnp.zeros((layers_here, shard_rows, width), jnp.float32)
    block_count = 4
    block_width = half // block_count
    inbox = jnp.zeros((shard_rows, 2 * block_width), jnp.float32)

    def step_blocks(step, carry):
        inbox, store_full, store_leave = carry
        block_num = step - member
        valid = (block_num >= 0) & (block_num < block_count)
        clipped = jnp.clip(block_num, 0, block_count - 1)
        source = jnp.where(member == 0, pick_block(start_amps, clipped, block_width, half), inbox)
        fulls, leaves = advance(source, interface, angle, decay)
        store_full = jnp.where(
            valid, put_block(store_full, fulls, clipped, block_width, half), store_full
        )
        store_leave = jnp.where(
            valid, put_block(store_leave, leaves, clipped, block_width, half), store_leave
        )
        inbox = shifted(leaves[layers_here - 1], "layer", 1)
        return (inbox, store_full, store_leave)

    inbox, store_full, store_leave = lax.fori_loop(
        0, groups + block_count - 1, step_blocks, (inbox, store_full, store_leave)
    )
    fields = []
    for layer_num in range(layers_here):
        depth = jnp.concatenate(
            [
                rotate(
                    store_full[layer_num], angle[layer_num], decay[layer_num], step / DEPTHS
                ).astype(jnp.bfloat16)
                for step in range(DEPTHS)
            ],
            axis=1,
        )
        fields.append(
            jnp.dot(eigvec[layer_num], depth, preferred_element_type=jnp.float32).astype(
                jnp.bfloat16
            )
        )
    return (jnp.stack(fields), store_leave)


def solution(mesh):
    in_specs = (
        P("tile", None),
        P("layer", "tile", None),
        P("layer", "tile", None),
        P("layer", None),
        P("layer", None),
    )
    out_specs = (P("layer", "tile", None), P("layer", "tile", None))
    return jax.shard_map(
        on_device, mesh=mesh, in_specs=in_specs, out_specs=out_specs, check_vma=False
    )
```

profile of v0, /device:TPU:1, one launch (start us, length us, event | category | flops | bytes accessed | tf_op | source)
XLA Modules:
  0.0 704.2 jit_solution(1159093125117101727)
XLA Ops:
  11.3 665.6 %while.20 = (s32[]{:T(128)}, f32[1024,32]{0,1:T(8,128)S(1)}, f32[2,4096,128]{1,2,0:T(8,128)}, f32[2,1024,128]{1,2,0:T(8,128)S(1)}, f32[2,4096]{1,0:T(2,128)}, /*...) while((s32[]{:T(128)}, f32[1024,32]{0,1:T(8,128)S(1)}, ...), condition=%wide.region_1.2_spmd.clone, body=%wide.region_0.1_spmd.clone.sunk | while | flops 543318016 | bytes 56263120 | solution.py:88
  12.3 15.3 %all_gather.24 = f32[4096,32]{0,1:T(8,128)S(1)} all-gather(f32[1024,32]{0,1:T(8,128)S(1)} %maximum_select_fusion.2), channel_id=1, replica_groups=mesh['layer'=8,'tile'=4] {'tile'}, dimensions={0}, use_global_device_ids=true | all-gather | bytes 655360 | tf_op jit(solution)/shard_map/while/body/eval_jaxpr/all_gather | solution.py:31
  34.4 11.9 %all_gather.25 = f32[4096,32]{0,1:T(8,128)S(1)} all-gather(f32[1024,32]{0,1:T(8,128)S(1)} %bitcast.104), channel_id=1, replica_groups=mesh['layer'=8,'tile'=4] {'tile'}, dimensions={0}, use_global_device_ids=true | all-gather | bytes 655360 | tf_op jit(solution)/shard_map/while/body/eval_jaxpr/all_gather | solution.py:31
  53.0 9.5 %collective-permute-start = (f32[1024,32]{0,1:T(8,128)S(1)}, f32[1024,32]{0,1:T(8,128)S(1)}, u32[]{:S(2)}, u32[]{:S(2)}) collective-permute-start(f32[1024,32]{0,1:T(8,128)S(1)} %bitcast.107), channel_id=1, source_target_pairs={{0,4},{4,8},{8,12},{12,16},{16,20},{20,24},{24,28},{1,5},{5,9},{9,... | collective-permute-start | bytes 393224 | tf_op jit(solution)/shard_map/while/body/eval_jaxpr/ppermute | solution.py:12
  71.0 13.6 %all_gather.24 = f32[4096,32]{0,1:T(8,128)S(1)} all-gather(f32[1024,32]{0,1:T(8,128)S(1)} %maximum_select_fusion.2), channel_id=1, replica_groups=mesh['layer'=8,'tile'=4] {'tile'}, dimensions={0}, use_global_device_ids=true | all-gather | bytes 655360 | tf_op jit(solution)/shard_map/while/body/eval_jaxpr/all_gather | solution.py:31
  91.3 11.9 %all_gather.25 = f32[4096,32]{0,1:T(8,128)S(1)} all-gather(f32[1024,32]{0,1:T(8,128)S(1)} %bitcast.104), channel_id=1, replica_groups=mesh['layer'=8,'tile'=4] {'tile'}, dimensions={0}, use_global_device_ids=true | all-gather | bytes 655360 | tf_op jit(solution)/shard_map/while/body/eval_jaxpr/all_gather | solution.py:31
  109.9 8.0 %collective-permute-start = (f32[1024,32]{0,1:T(8,128)S(1)}, f32[1024,32]{0,1:T(8,128)S(1)}, u32[]{:S(2)}, u32[]{:S(2)}) collective-permute-start(f32[1024,32]{0,1:T(8,128)S(1)} %bitcast.107), channel_id=1, source_target_pairs={{0,4},{4,8},{8,12},{12,16},{16,20},{20,24},{24,28},{1,5},{5,9},{9,... | collective-permute-start | bytes 393224 | tf_op jit(solution)/shard_map/while/body/eval_jaxpr/ppermute | solution.py:12
  132.1 14.9 %all_gather.24 = f32[4096,32]{0,1:T(8,128)S(1)} all-gather(f32[1024,32]{0,1:T(8,128)S(1)} %maximum_select_fusion.2), channel_id=1, replica_groups=mesh['layer'=8,'tile'=4] {'tile'}, dimensions={0}, use_global_device_ids=true | all-gather | bytes 655360 | tf_op jit(solution)/shard_map/while/body/eval_jaxpr/all_gather | solution.py:31
  153.7 14.3 %all_gather.25 = f32[4096,32]{0,1:T(8,128)S(1)} all-gather(f32[1024,32]{0,1:T(8,128)S(1)} %bitcast.104), channel_id=1, replica_groups=mesh['layer'=8,'tile'=4] {'tile'}, dimensions={0}, use_global_device_ids=true | all-gather | bytes 655360 | tf_op jit(solution)/shard_map/while/body/eval_jaxpr/all_gather | solution.py:31
  193.1 15.5 %all_gather.24 = f32[4096,32]{0,1:T(8,128)S(1)} all-gather(f32[1024,32]{0,1:T(8,128)S(1)} %maximum_select_fusion.2), channel_id=1, replica_groups=mesh['layer'=8,'tile'=4] {'tile'}, dimensions={0}, use_global_device_ids=true | all-gather | bytes 655360 | tf_op jit(solution)/shard_map/while/body/eval_jaxpr/all_gather | solution.py:31
  215.4 13.9 %all_gather.25 = f32[4096,32]{0,1:T(8,128)S(1)} all-gather(f32[1024,32]{0,1:T(8,128)S(1)} %bitcast.104), channel_id=1, replica_groups=mesh['layer'=8,'tile'=4] {'tile'}, dimensions={0}, use_global_device_ids=true | all-gather | bytes 655360 | tf_op jit(solution)/shard_map/while/body/eval_jaxpr/all_gather | solution.py:31
  255.2 14.3 %all_gather.24 = f32[4096,32]{0,1:T(8,128)S(1)} all-gather(f32[1024,32]{0,1:T(8,128)S(1)} %maximum_select_fusion.2), channel_id=1, replica_groups=mesh['layer'=8,'tile'=4] {'tile'}, dimensions={0}, use_global_device_ids=true | all-gather | bytes 655360 | tf_op jit(solution)/shard_map/while/body/eval_jaxpr/all_gather | solution.py:31
  276.2 13.6 %all_gather.25 = f32[4096,32]{0,1:T(8,128)S(1)} all-gather(f32[1024,32]{0,1:T(8,128)S(1)} %bitcast.104), channel_id=1, replica_groups=mesh['layer'=8,'tile'=4] {'tile'}, dimensions={0}, use_global_device_ids=true | all-gather | bytes 655360 | tf_op jit(solution)/shard_map/while/body/eval_jaxpr/all_gather | solution.py:31
  316.4 14.3 %all_gather.24 = f32[4096,32]{0,1:T(8,128)S(1)} all-gather(f32[1024,32]{0,1:T(8,128)S(1)} %maximum_select_fusion.2), channel_id=1, replica_groups=mesh['layer'=8,'tile'=4] {'tile'}, dimensions={0}, use_global_device_ids=true | all-gather | bytes 655360 | tf_op jit(solution)/shard_map/while/body/eval_jaxpr/all_gather | solution.py:31
  337.4 13.9 %all_gather.25 = f32[4096,32]{0,1:T(8,128)S(1)} all-gather(f32[1024,32]{0,1:T(8,128)S(1)} %bitcast.104), channel_id=1, replica_groups=mesh['layer'=8,'tile'=4] {'tile'}, dimensions={0}, use_global_device_ids=true | all-gather | bytes 655360 | tf_op jit(solution)/shard_map/while/body/eval_jaxpr/all_gather | solution.py:31
  376.7 13.5 %all_gather.24 = f32[4096,32]{0,1:T(8,128)S(1)} all-gather(f32[1024,32]{0,1:T(8,128)S(1)} %maximum_select_fusion.2), channel_id=1, replica_groups=mesh['layer'=8,'tile'=4] {'tile'}, dimensions={0}, use_global_device_ids=true | all-gather | bytes 655360 | tf_op jit(solution)/shard_map/while/body/eval_jaxpr/all_gather | solution.py:31
  397.0 13.6 %all_gather.25 = f32[4096,32]{0,1:T(8,128)S(1)} all-gather(f32[1024,32]{0,1:T(8,128)S(1)} %bitcast.104), channel_id=1, replica_groups=mesh['layer'=8,'tile'=4] {'tile'}, dimensions={0}, use_global_device_ids=true | all-gather | bytes 655360 | tf_op jit(solution)/shard_map/while/body/eval_jaxpr/all_gather | solution.py:31
  417.3 7.9 %collective-permute-start = (f32[1024,32]{0,1:T(8,128)S(1)}, f32[1024,32]{0,1:T(8,128)S(1)}, u32[]{:S(2)}, u32[]{:S(2)}) collective-permute-start(f32[1024,32]{0,1:T(8,128)S(1)} %bitcast.107), channel_id=1, source_target_pairs={{0,4},{4,8},{8,12},{12,16},{16,20},{20,24},{24,28},{1,5},{5,9},{9,... | collective-permute-start | bytes 393224 | tf_op jit(solution)/shard_map/while/body/eval_jaxpr/ppermute | solution.py:12
  438.2 12.0 %all_gather.24 = f32[4096,32]{0,1:T(8,128)S(1)} all-gather(f32[1024,32]{0,1:T(8,128)S(1)} %maximum_select_fusion.2), channel_id=1, replica_groups=mesh['layer'=8,'tile'=4] {'tile'}, dimensions={0}, use_global_device_ids=true | all-gather | bytes 655360 | tf_op jit(solution)/shard_map/while/body/eval_jaxpr/all_gather | solution.py:31
  456.9 14.2 %all_gather.25 = f32[4096,32]{0,1:T(8,128)S(1)} all-gather(f32[1024,32]{0,1:T(8,128)S(1)} %bitcast.104), channel_id=1, replica_groups=mesh['layer'=8,'tile'=4] {'tile'}, dimensions={0}, use_global_device_ids=true | all-gather | bytes 655360 | tf_op jit(solution)/shard_map/while/body/eval_jaxpr/all_gather | solution.py:31
  477.9 7.3 %collective-permute-start = (f32[1024,32]{0,1:T(8,128)S(1)}, f32[1024,32]{0,1:T(8,128)S(1)}, u32[]{:S(2)}, u32[]{:S(2)}) collective-permute-start(f32[1024,32]{0,1:T(8,128)S(1)} %bitcast.107), channel_id=1, source_target_pairs={{0,4},{4,8},{8,12},{12,16},{16,20},{20,24},{24,28},{1,5},{5,9},{9,... | collective-permute-start | bytes 393224 | tf_op jit(solution)/shard_map/while/body/eval_jaxpr/ppermute | solution.py:12
  498.2 12.1 %all_gather.24 = f32[4096,32]{0,1:T(8,128)S(1)} all-gather(f32[1024,32]{0,1:T(8,128)S(1)} %maximum_select_fusion.2), channel_id=1, replica_groups=mesh['layer'=8,'tile'=4] {'tile'}, dimensions={0}, use_global_device_ids=true | all-gather | bytes 655360 | tf_op jit(solution)/shard_map/while/body/eval_jaxpr/all_gather | solution.py:31
  517.0 14.0 %all_gather.25 = f32[4096,32]{0,1:T(8,128)S(1)} all-gather(f32[1024,32]{0,1:T(8,128)S(1)} %bitcast.104), channel_id=1, replica_groups=mesh['layer'=8,'tile'=4] {'tile'}, dimensions={0}, use_global_device_ids=true | all-gather | bytes 655360 | tf_op jit(solution)/shard_map/while/body/eval_jaxpr/all_gather | solution.py:31
  537.8 7.2 %collective-permute-start = (f32[1024,32]{0,1:T(8,128)S(1)}, f32[1024,32]{0,1:T(8,128)S(1)}, u32[]{:S(2)}, u32[]{:S(2)}) collective-permute-start(f32[1024,32]{0,1:T(8,128)S(1)} %bitcast.107), channel_id=1, source_target_pairs={{0,4},{4,8},{8,12},{12,16},{16,20},{20,24},{24,28},{1,5},{5,9},{9,... | collective-permute-start | bytes 393224 | tf_op jit(solution)/shard_map/while/body/eval_jaxpr/ppermute | solution.py:12
  558.0 12.3 %all_gather.24 = f32[4096,32]{0,1:T(8,128)S(1)} all-gather(f32[1024,32]{0,1:T(8,128)S(1)} %maximum_select_fusion.2), channel_id=1, replica_groups=mesh['layer'=8,'tile'=4] {'tile'}, dimensions={0}, use_global_device_ids=true | all-gather | bytes 655360 | tf_op jit(solution)/shard_map/while/body/eval_jaxpr/all_gather | solution.py:31
  577.1 13.9 %all_gather.25 = f32[4096,32]{0,1:T(8,128)S(1)} all-gather(f32[1024,32]{0,1:T(8,128)S(1)} %bitcast.104), channel_id=1, replica_groups=mesh['layer'=8,'tile'=4] {'tile'}, dimensions={0}, use_global_device_ids=true | all-gather | bytes 655360 | tf_op jit(solution)/shard_map/while/body/eval_jaxpr/all_gather | solution.py:31
  597.8 7.2 %collective-permute-start = (f32[1024,32]{0,1:T(8,128)S(1)}, f32[1024,32]{0,1:T(8,128)S(1)}, u32[]{:S(2)}, u32[]{:S(2)}) collective-permute-start(f32[1024,32]{0,1:T(8,128)S(1)} %bitcast.107), channel_id=1, source_target_pairs={{0,4},{4,8},{8,12},{12,16},{16,20},{20,24},{24,28},{1,5},{5,9},{9,... | collective-permute-start | bytes 393224 | tf_op jit(solution)/shard_map/while/body/eval_jaxpr/ppermute | solution.py:12
  617.9 12.3 %all_gather.24 = f32[4096,32]{0,1:T(8,128)S(1)} all-gather(f32[1024,32]{0,1:T(8,128)S(1)} %maximum_select_fusion.2), channel_id=1, replica_groups=mesh['layer'=8,'tile'=4] {'tile'}, dimensions={0}, use_global_device_ids=true | all-gather | bytes 655360 | tf_op jit(solution)/shard_map/while/body/eval_jaxpr/all_gather | solution.py:31
  636.9 14.3 %all_gather.25 = f32[4096,32]{0,1:T(8,128)S(1)} all-gather(f32[1024,32]{0,1:T(8,128)S(1)} %bitcast.104), channel_id=1, replica_groups=mesh['layer'=8,'tile'=4] {'tile'}, dimensions={0}, use_global_device_ids=true | all-gather | bytes 655360 | tf_op jit(solution)/shard_map/while/body/eval_jaxpr/all_gather | solution.py:31
  658.0 6.9 collective-permute-start
  685.7 7.3 %fusion.35 = bf16[1,1024,512]{1,2,0:T(8,128)(2,1)S(1)} fusion(bf16[4096,512]{0,1:T(8,128)(2,1)S(1)} %fusion.45, bf16[2,1024,4096]{2,1,0:T(8,128)(2,1)} %param.9), kind=kOutput, calls=%fused_computation.51 | convolution fusion | flops 4295491584 | bytes 13631488 | tf_op jit(solution)/shard_map/dot_general | solution.py:103
  694.4 7.1 %fusion.32 = bf16[1,1024,512]{1,2,0:T(8,128)(2,1)S(1)} fusion(bf16[4096,512]{0,1:T(8,128)(2,1)S(1)} %fusion.53, bf16[2,1024,4096]{2,1,0:T(8,128)(2,1)} %param.9), kind=kOutput, calls=%fused_computation.50 | convolution fusion | flops 4295491584 | bytes 13631488 | tf_op jit(solution)/shard_map/dot_general | solution.py:103
  (306 shorter events, 333.8 us)
Async XLA Ops:
  11.3 1.0 copy-start.1
  53.0 16.9 %collective-permute-start = (f32[1024,32]{0,1:T(8,128)S(1)}, f32[1024,32]{0,1:T(8,128)S(1)}, u32[]{:S(2)}, u32[]{:S(2)}) collective-permute-start(f32[1024,32]{0,1:T(8,128)S(1)} %bitcast.107), channel_id=1, source_target_pairs={{0,4},{4,8},{8,12},{12,16},{16,20},{20,24},{24,28},{1,5},{5,9},{9,... | collective-permute-start | bytes 393224 | tf_op jit(solution)/shard_map/while/body/eval_jaxpr/ppermute | solution.py:12
  66.8 3.1 copy-start.2
  109.9 21.1 %collective-permute-start = (f32[1024,32]{0,1:T(8,128)S(1)}, f32[1024,32]{0,1:T(8,128)S(1)}, u32[]{:S(2)}, u32[]{:S(2)}) collective-permute-start(f32[1024,32]{0,1:T(8,128)S(1)} %bitcast.107), channel_id=1, source_target_pairs={{0,4},{4,8},{8,12},{12,16},{16,20},{20,24},{24,28},{1,5},{5,9},{9,... | collective-permute-start | bytes 393224 | tf_op jit(solution)/shard_map/while/body/eval_jaxpr/ppermute | solution.py:12
  124.4 6.6 copy-start.2
  174.8 17.3 %collective-permute-start = (f32[1024,32]{0,1:T(8,128)S(1)}, f32[1024,32]{0,1:T(8,128)S(1)}, u32[]{:S(2)}, u32[]{:S(2)}) collective-permute-start(f32[1024,32]{0,1:T(8,128)S(1)} %bitcast.107), channel_id=1, source_target_pairs={{0,4},{4,8},{8,12},{12,16},{16,20},{20,24},{24,28},{1,5},{5,9},{9,... | collective-permute-start | bytes 393224 | tf_op jit(solution)/shard_map/while/body/eval_jaxpr/ppermute | solution.py:12
  185.5 6.6 copy-start.2
  236.1 18.1 %collective-permute-start = (f32[1024,32]{0,1:T(8,128)S(1)}, f32[1024,32]{0,1:T(8,128)S(1)}, u32[]{:S(2)}, u32[]{:S(2)}) collective-permute-start(f32[1024,32]{0,1:T(8,128)S(1)} %bitcast.107), channel_id=1, source_target_pairs={{0,4},{4,8},{8,12},{12,16},{16,20},{20,24},{24,28},{1,5},{5,9},{9,... | collective-permute-start | bytes 393224 | tf_op jit(solution)/shard_map/while/body/eval_jaxpr/ppermute | solution.py:12
  247.6 6.6 copy-start.2
  296.6 18.7 %collective-permute-start = (f32[1024,32]{0,1:T(8,128)S(1)}, f32[1024,32]{0,1:T(8,128)S(1)}, u32[]{:S(2)}, u32[]{:S(2)}) collective-permute-start(f32[1024,32]{0,1:T(8,128)S(1)} %bitcast.107), channel_id=1, source_target_pairs={{0,4},{4,8},{8,12},{12,16},{16,20},{20,24},{24,28},{1,5},{5,9},{9,... | collective-permute-start | bytes 393224 | tf_op jit(solution)/shard_map/while/body/eval_jaxpr/ppermute | solution.py:12
  308.7 6.6 copy-start.2
  358.0 17.6 %collective-permute-start = (f32[1024,32]{0,1:T(8,128)S(1)}, f32[1024,32]{0,1:T(8,128)S(1)}, u32[]{:S(2)}, u32[]{:S(2)}) collective-permute-start(f32[1024,32]{0,1:T(8,128)S(1)} %bitcast.107), channel_id=1, source_target_pairs={{0,4},{4,8},{8,12},{12,16},{16,20},{20,24},{24,28},{1,5},{5,9},{9,... | collective-permute-start | bytes 393224 | tf_op jit(solution)/shard_map/while/body/eval_jaxpr/ppermute | solution.py:12
  370.3 5.3 copy-start.2
  417.3 19.8 %collective-permute-start = (f32[1024,32]{0,1:T(8,128)S(1)}, f32[1024,32]{0,1:T(8,128)S(1)}, u32[]{:S(2)}, u32[]{:S(2)}) collective-permute-start(f32[1024,32]{0,1:T(8,128)S(1)} %bitcast.107), channel_id=1, source_target_pairs={{0,4},{4,8},{8,12},{12,16},{16,20},{20,24},{24,28},{1,5},{5,9},{9,... | collective-permute-start | bytes 393224 | tf_op jit(solution)/shard_map/while/body/eval_jaxpr/ppermute | solution.py:12
  431.8 5.3 copy-start.2
  477.9 19.2 %collective-permute-start = (f32[1024,32]{0,1:T(8,128)S(1)}, f32[1024,32]{0,1:T(8,128)S(1)}, u32[]{:S(2)}, u32[]{:S(2)}) collective-permute-start(f32[1024,32]{0,1:T(8,128)S(1)} %bitcast.107), channel_id=1, source_target_pairs={{0,4},{4,8},{8,12},{12,16},{16,20},{20,24},{24,28},{1,5},{5,9},{9,... | collective-permute-start | bytes 393224 | tf_op jit(solution)/shard_map/while/body/eval_jaxpr/ppermute | solution.py:12
  491.8 5.3 copy-start.2
  537.8 19.1 %collective-permute-start = (f32[1024,32]{0,1:T(8,128)S(1)}, f32[1024,32]{0,1:T(8,128)S(1)}, u32[]{:S(2)}, u32[]{:S(2)}) collective-permute-start(f32[1024,32]{0,1:T(8,128)S(1)} %bitcast.107), channel_id=1, source_target_pairs={{0,4},{4,8},{8,12},{12,16},{16,20},{20,24},{24,28},{1,5},{5,9},{9,... | collective-permute-start | bytes 393224 | tf_op jit(solution)/shard_map/while/body/eval_jaxpr/ppermute | solution.py:12
  551.6 5.3 copy-start.2
  597.8 19.1 %collective-permute-start = (f32[1024,32]{0,1:T(8,128)S(1)}, f32[1024,32]{0,1:T(8,128)S(1)}, u32[]{:S(2)}, u32[]{:S(2)}) collective-permute-start(f32[1024,32]{0,1:T(8,128)S(1)} %bitcast.107), channel_id=1, source_target_pairs={{0,4},{4,8},{8,12},{12,16},{16,20},{20,24},{24,28},{1,5},{5,9},{9,... | collective-permute-start | bytes 393224 | tf_op jit(solution)/shard_map/while/body/eval_jaxpr/ppermute | solution.py:12
  611.6 5.3 copy-start.2
  658.0 18.9 %collective-permute-start = (f32[1024,32]{0,1:T(8,128)S(1)}, f32[1024,32]{0,1:T(8,128)S(1)}, u32[]{:S(2)}, u32[]{:S(2)}) collective-permute-start(f32[1024,32]{0,1:T(8,128)S(1)} %bitcast.107), channel_id=1, source_target_pairs={{0,4},{4,8},{8,12},{12,16},{16,20},{20,24},{24,28},{1,5},{5,9},{9,... | collective-permute-start | bytes 393224 | tf_op jit(solution)/shard_map/while/body/eval_jaxpr/ppermute | solution.py:12
  671.5 5.3 copy-start.2
  676.9 5.3 copy-start.15
  676.9 5.3 copy-start.16
  676.9 5.3 copy-start.17
  676.9 5.3 copy-start.18
  682.2 2.2 copy-start
  682.2 2.4 copy-start.13
  682.2 2.4 copy-start.14
  685.7 7.5 %copy-start.4 = (f32[1,4096]{1,0:T(1,128)S(1)}, f32[1,4096]{1,0:T(1,128)}, u32[]{:S(2)}) copy-start(f32[1,4096]{1,0:T(1,128)} %get-tuple-element.339) | copy-start | bytes 49156
  685.7 7.5 %copy-start.8 = (f32[1,4096]{1,0:T(1,128)S(1)}, f32[1,4096]{1,0:T(1,128)}, u32[]{:S(2)}) copy-start(f32[1,4096]{1,0:T(1,128)} %get-tuple-element.344) | copy-start | bytes 49156
  (18 other events, 15.7 us)
where the time goes:
time: 709 us; the launch traced here: 704 us
  blocking collectives  300 us (42%)
  other arithmetic  173 us (24%)
  matrix products  145 us (20%)
  starting transfers between devices  74.1 us (10%)
  local copies, waits for them, and re-layouts  9.94 us (1%)
    all_gather x22, blocking collectives, advance(): full = lax.all_gather(current, 'tile', axis=0, tiled=True)  300 us
    dot_general x22, matrix products, advance(): jnp.dot(interface[layer_num], phased, preferred_element_type=jnp.float32)  131 us
    ppermute x11, starting transfers between devices, shifted(): return lax.ppermute(x, axis, pairs)  74.1 us
    select_n x11, other arithmetic, step_blocks(): jnp.where(valid, put_block(store_full, fulls, clipped, block_width, half)...  57.7 us
    while x22, other arithmetic  50.2 us
    mul x24, other arithmetic, rotate(): cosine = (scale * jnp.cos(frac * angle_row))[:, None]  25.5 us
    dot_general x2, matrix products, on_device(): jnp.dot(eigvec[layer_num], depth, preferred_element_type=jnp.float32)  14.4 us
  transfers between devices with their start and end apart: 11, of which 0 were waited for; matrix products, arithmetic and copies ran while one was open for 19% of the time, Pallas kernels for 0%

commit v1 on v0

--- a/solution.py
+++ b/solution.py
@@ -28,7 +28,9 @@
     fulls = []
     leaves = []
     for layer_num in range(interface.shape[0]):
-        full = lax.all_gather(current, "tile", axis=0, tiled=True)
+        full = jnp.concatenate(
+            lax.all_to_all(jnp.stack([current] * lax.axis_size("tile")), "tile", 0, 0), axis=0
+        )
         fulls.append(full)
         phased = rotate(full, angle[layer_num], decay[layer_num], 1.0).astype(jnp.bfloat16)
         current = jnp.dot(interface[layer_num], phased, preferred_element_type=jnp.float32)

time: 709 us -> 758 us (1.069)
  blocking collectives: 300 us -> 0 us
  waiting for transfers between devices: 0.03 us -> 206 us
  local copies, waits for them, and re-layouts: 9.94 us -> 146 us
  starting transfers between devices: 74.1 us -> 106 us
  other arithmetic: 173 us -> 145 us
    all_gather x22 -> x0, blocking collectives: 300 us -> none  [advance(): full = lax.all_gather(current, 'tile', axis=0, tiled=True)]
    all_to_all x0 -> x22, waiting for transfers between devices: none -> 206 us  [advance(): lax.all_to_all(jnp.stack([current] * lax.axis_size('tile')), 'tile', 0, 0)]
    all_to_all x0 -> x22, starting transfers between devices: none -> 78.3 us  [advance(): lax.all_to_all(jnp.stack([current] * lax.axis_size('tile')), 'tile', 0, 0)]
    ppermute x11, starting transfers between devices: 74.1 us -> 27.4 us  [shifted(): return lax.ppermute(x, axis, pairs)]
    dynamic_update_slice x0 -> x22, local copies, waits for them, and re-layouts: none -> 41.6 us  [the longest x11 20.8 us: put_block(): lax.dynamic_update_slice_in_dim(values, real_piece, block_num * block_wid...]
    reshape x0 -> x44, local copies, waits for them, and re-layouts: none -> 31.7 us  [the longest x22 30.8 us: advance(): return (jnp.stack(fulls), jnp.stack(leaves))]
    another operation x0 -> x33, local copies, waits for them, and re-layouts: none -> 28.3 us  [the longest x22 19.1 us: advance(): jnp.stack([current] * lax.axis_size('tile'))]
    all_to_all x0 -> x22, local copies, waits for them, and re-layouts: none -> 25 us  [advance(): lax.all_to_all(jnp.stack([current] * lax.axis_size('tile')), 'tile', 0, 0)]
  transfers between devices with their start and end apart: 11 -> 33, of which waited for: 0 -> 22; matrix products, arithmetic and copies ran while one was open for 19% -> 33% of each run, Pallas kernels for 0% -> 0%
where the time goes in v1:
time: 758 us; the launch traced here: 751 us
  waiting for transfers between devices  206 us (27%)
  local copies, waits for them, and re-layouts  146 us (19%)
  other arithmetic  145 us (19%)
  matrix products  145 us (19%)
  starting transfers between devices  106 us (14%)
    all_to_all x22, waiting for transfers between devices, advance(): lax.all_to_all(jnp.stack([current] * lax.axis_size('tile')), 'tile', 0, 0)  206 us
    dot_general x22, matrix products, advance(): jnp.dot(interface[layer_num], phased, preferred_element_type=jnp.float32)  131 us
    all_to_all x22, starting transfers between devices, advance(): lax.all_to_all(jnp.stack([current] * lax.axis_size('tile')), 'tile', 0, 0)  78.3 us
    select_n x11, other arithmetic, step_blocks(): jnp.where(valid, put_block(store_full, fulls, clipped, block_width, half)...  58.6 us
    while x22, other arithmetic  49.5 us
    reshape x22, local copies, waits for them, and re-layouts, advance(): return (jnp.stack(fulls), jnp.stack(leaves))  30.8 us
    ppermute x11, starting transfers between devices, shifted(): return lax.ppermute(x, axis, pairs)  27.4 us
    all_to_all x22, local copies, waits for them, and re-layouts, advance(): lax.all_to_all(jnp.stack([current] * lax.axis_size('tile')), 'tile', 0, 0)  25 us
  transfers between devices with their start and end apart: 33, of which 22 were waited for; matrix products, arithmetic and copies ran while one was open for 33% of the time, Pallas kernels for 0%

profile of v1, /device:TPU:1, one launch (start us, length us, event | category | flops | bytes accessed | tf_op | source)
XLA Modules:
  0.0 751.1 jit_solution(8185279228357362888)
XLA Ops:
  11.2 712.4 %while.20 = (s32[]{:T(128)}, f32[1024,32]{0,1:T(8,128)S(1)}, f32[2,4096,128]{1,2,0:T(8,128)}, f32[2,1024,128]{1,2,0:T(8,128)S(1)}, f32[2,4096]{1,0:T(2,128)}, /*...) while((s32[]{:T(128)}, f32[1024,32]{0,1:T(8,128)S(1)}, ...), condition=%wide.region_1.2_spmd.clone, body=%wide.region_0.1_spmd.clone.sunk | while | flops 543055872 | bytes 66880072 | solution.py:90
  21.0 10.7 %all-to-all-done = f32[4,1024,32]{1,2,0:T(8,128)S(1)} async-done(((f32[4,1024,32]{1,2,0:T(8,128)}), f32[4,1024,32]{1,2,0:T(8,128)S(1)}, u32[]{:S(2)}, u32[]{:S(2)}) %all-to-all-start) | async-done | bytes 524320 | tf_op jit(solution)/shard_map/while/body/eval_jaxpr/all_to_all | solution.py:32
  46.3 9.8 %all-to-all-done.1 = f32[4,1024,32]{1,2,0:T(8,128)S(1)} async-done(((f32[4,1024,32]{1,2,0:T(8,128)}), f32[4,1024,32]{1,2,0:T(8,128)S(1)}, u32[]{:S(2)}, u32[]{:S(2)}) %all-to-all-start.1) | async-done | bytes 524320 | tf_op jit(solution)/shard_map/while/body/eval_jaxpr/all_to_all | solution.py:32
  87.0 8.5 %all-to-all-done = f32[4,1024,32]{1,2,0:T(8,128)S(1)} async-done(((f32[4,1024,32]{1,2,0:T(8,128)}), f32[4,1024,32]{1,2,0:T(8,128)S(1)}, u32[]{:S(2)}, u32[]{:S(2)}) %all-to-all-start) | async-done | bytes 524320 | tf_op jit(solution)/shard_map/while/body/eval_jaxpr/all_to_all | solution.py:32
  110.2 9.8 %all-to-all-done.1 = f32[4,1024,32]{1,2,0:T(8,128)S(1)} async-done(((f32[4,1024,32]{1,2,0:T(8,128)}), f32[4,1024,32]{1,2,0:T(8,128)S(1)}, u32[]{:S(2)}, u32[]{:S(2)}) %all-to-all-start.1) | async-done | bytes 524320 | tf_op jit(solution)/shard_map/while/body/eval_jaxpr/all_to_all | solution.py:32
  137.7 6.3 broadcast_select_fusion.9
  154.4 7.9 %all-to-all-done = f32[4,1024,32]{1,2,0:T(8,128)S(1)} async-done(((f32[4,1024,32]{1,2,0:T(8,128)}), f32[4,1024,32]{1,2,0:T(8,128)S(1)}, u32[]{:S(2)}, u32[]{:S(2)}) %all-to-all-start) | async-done | bytes 524320 | tf_op jit(solution)/shard_map/while/body/eval_jaxpr/all_to_all | solution.py:32
  176.9 10.6 %all-to-all-done.1 = f32[4,1024,32]{1,2,0:T(8,128)S(1)} async-done(((f32[4,1024,32]{1,2,0:T(8,128)}), f32[4,1024,32]{1,2,0:T(8,128)S(1)}, u32[]{:S(2)}, u32[]{:S(2)}) %all-to-all-start.1) | async-done | bytes 524320 | tf_op jit(solution)/shard_map/while/body/eval_jaxpr/all_to_all | solution.py:32
  203.8 6.3 broadcast_select_fusion.9
  220.5 9.2 %all-to-all-done = f32[4,1024,32]{1,2,0:T(8,128)S(1)} async-done(((f32[4,1024,32]{1,2,0:T(8,128)}), f32[4,1024,32]{1,2,0:T(8,128)S(1)}, u32[]{:S(2)}, u32[]{:S(2)}) %all-to-all-start) | async-done | bytes 524320 | tf_op jit(solution)/shard_map/while/body/eval_jaxpr/all_to_all | solution.py:32
  244.3 9.9 %all-to-all-done.1 = f32[4,1024,32]{1,2,0:T(8,128)S(1)} async-done(((f32[4,1024,32]{1,2,0:T(8,128)}), f32[4,1024,32]{1,2,0:T(8,128)S(1)}, u32[]{:S(2)}, u32[]{:S(2)}) %all-to-all-start.1) | async-done | bytes 524320 | tf_op jit(solution)/shard_map/while/body/eval_jaxpr/all_to_all | solution.py:32
  254.4 6.0 fusion.72
  269.4 6.3 broadcast_select_fusion.9
  286.1 8.5 %all-to-all-done = f32[4,1024,32]{1,2,0:T(8,128)S(1)} async-done(((f32[4,1024,32]{1,2,0:T(8,128)}), f32[4,1024,32]{1,2,0:T(8,128)S(1)}, u32[]{:S(2)}, u32[]{:S(2)}) %all-to-all-start) | async-done | bytes 524320 | tf_op jit(solution)/shard_map/while/body/eval_jaxpr/all_to_all | solution.py:32
  309.2 9.8 %all-to-all-done.1 = f32[4,1024,32]{1,2,0:T(8,128)S(1)} async-done(((f32[4,1024,32]{1,2,0:T(8,128)}), f32[4,1024,32]{1,2,0:T(8,128)S(1)}, u32[]{:S(2)}, u32[]{:S(2)}) %all-to-all-start.1) | async-done | bytes 524320 | tf_op jit(solution)/shard_map/while/body/eval_jaxpr/all_to_all | solution.py:32
  319.1 6.0 fusion.72
  334.3 6.3 broadcast_select_fusion.9
  350.9 9.5 %all-to-all-done = f32[4,1024,32]{1,2,0:T(8,128)S(1)} async-done(((f32[4,1024,32]{1,2,0:T(8,128)}), f32[4,1024,32]{1,2,0:T(8,128)S(1)}, u32[]{:S(2)}, u32[]{:S(2)}) %all-to-all-start) | async-done | bytes 524320 | tf_op jit(solution)/shard_map/while/body/eval_jaxpr/all_to_all | solution.py:32
  375.0 9.9 %all-to-all-done.1 = f32[4,1024,32]{1,2,0:T(8,128)S(1)} async-done(((f32[4,1024,32]{1,2,0:T(8,128)}), f32[4,1024,32]{1,2,0:T(8,128)S(1)}, u32[]{:S(2)}, u32[]{:S(2)}) %all-to-all-start.1) | async-done | bytes 524320 | tf_op jit(solution)/shard_map/while/body/eval_jaxpr/all_to_all | solution.py:32
  385.1 6.0 fusion.72
  415.6 8.5 %all-to-all-done = f32[4,1024,32]{1,2,0:T(8,128)S(1)} async-done(((f32[4,1024,32]{1,2,0:T(8,128)}), f32[4,1024,32]{1,2,0:T(8,128)S(1)}, u32[]{:S(2)}, u32[]{:S(2)}) %all-to-all-start) | async-done | bytes 524320 | tf_op jit(solution)/shard_map/while/body/eval_jaxpr/all_to_all | solution.py:32
  438.8 9.8 %all-to-all-done.1 = f32[4,1024,32]{1,2,0:T(8,128)S(1)} async-done(((f32[4,1024,32]{1,2,0:T(8,128)}), f32[4,1024,32]{1,2,0:T(8,128)S(1)}, u32[]{:S(2)}, u32[]{:S(2)}) %all-to-all-start.1) | async-done | bytes 524320 | tf_op jit(solution)/shard_map/while/body/eval_jaxpr/all_to_all | solution.py:32
  479.2 8.5 %all-to-all-done = f32[4,1024,32]{1,2,0:T(8,128)S(1)} async-done(((f32[4,1024,32]{1,2,0:T(8,128)}), f32[4,1024,32]{1,2,0:T(8,128)S(1)}, u32[]{:S(2)}, u32[]{:S(2)}) %all-to-all-start) | async-done | bytes 524320 | tf_op jit(solution)/shard_map/while/body/eval_jaxpr/all_to_all | solution.py:32
  502.3 9.8 %all-to-all-done.1 = f32[4,1024,32]{1,2,0:T(8,128)S(1)} async-done(((f32[4,1024,32]{1,2,0:T(8,128)}), f32[4,1024,32]{1,2,0:T(8,128)S(1)}, u32[]{:S(2)}, u32[]{:S(2)}) %all-to-all-start.1) | async-done | bytes 524320 | tf_op jit(solution)/shard_map/while/body/eval_jaxpr/all_to_all | solution.py:32
  542.8 8.5 %all-to-all-done = f32[4,1024,32]{1,2,0:T(8,128)S(1)} async-done(((f32[4,1024,32]{1,2,0:T(8,128)}), f32[4,1024,32]{1,2,0:T(8,128)S(1)}, u32[]{:S(2)}, u32[]{:S(2)}) %all-to-all-start) | async-done | bytes 524320 | tf_op jit(solution)/shard_map/while/body/eval_jaxpr/all_to_all | solution.py:32
  566.0 9.8 %all-to-all-done.1 = f32[4,1024,32]{1,2,0:T(8,128)S(1)} async-done(((f32[4,1024,32]{1,2,0:T(8,128)}), f32[4,1024,32]{1,2,0:T(8,128)S(1)}, u32[]{:S(2)}, u32[]{:S(2)}) %all-to-all-start.1) | async-done | bytes 524320 | tf_op jit(solution)/shard_map/while/body/eval_jaxpr/all_to_all | solution.py:32
  606.4 8.5 %all-to-all-done = f32[4,1024,32]{1,2,0:T(8,128)S(1)} async-done(((f32[4,1024,32]{1,2,0:T(8,128)}), f32[4,1024,32]{1,2,0:T(8,128)S(1)}, u32[]{:S(2)}, u32[]{:S(2)}) %all-to-all-start) | async-done | bytes 524320 | tf_op jit(solution)/shard_map/while/body/eval_jaxpr/all_to_all | solution.py:32
  629.6 9.8 %all-to-all-done.1 = f32[4,1024,32]{1,2,0:T(8,128)S(1)} async-done(((f32[4,1024,32]{1,2,0:T(8,128)}), f32[4,1024,32]{1,2,0:T(8,128)S(1)}, u32[]{:S(2)}, u32[]{:S(2)}) %all-to-all-start.1) | async-done | bytes 524320 | tf_op jit(solution)/shard_map/while/body/eval_jaxpr/all_to_all | solution.py:32
  670.0 8.5 %all-to-all-done = f32[4,1024,32]{1,2,0:T(8,128)S(1)} async-done(((f32[4,1024,32]{1,2,0:T(8,128)}), f32[4,1024,32]{1,2,0:T(8,128)S(1)}, u32[]{:S(2)}, u32[]{:S(2)}) %all-to-all-start) | async-done | bytes 524320 | tf_op jit(solution)/shard_map/while/body/eval_jaxpr/all_to_all | solution.py:32
  693.2 9.8 %all-to-all-done.1 = f32[4,1024,32]{1,2,0:T(8,128)S(1)} async-done(((f32[4,1024,32]{1,2,0:T(8,128)}), f32[4,1024,32]{1,2,0:T(8,128)S(1)}, u32[]{:S(2)}, u32[]{:S(2)}) %all-to-all-start.1) | async-done | bytes 524320 | tf_op jit(solution)/shard_map/while/body/eval_jaxpr/all_to_all | solution.py:32
  732.6 7.3 fusion.32
  741.2 7.1 fusion.29
  (482 shorter events, 484.7 us)
Async XLA Ops:
  12.2 19.5 %all-to-all-start = ((f32[4,1024,32]{1,2,0:T(8,128)}), f32[4,1024,32]{1,2,0:T(8,128)S(1)}, u32[]{:S(2)}, u32[]{:S(2)}) async-start(f32[4,1024,32]{1,2,0:T(8,128)} %stack.80), calls=%async_computation | async-start | bytes 1048576 | tf_op jit(solution)/shard_map/while/body/eval_jaxpr/all_to_all | solution.py:32
  38.6 17.5 %all-to-all-start.1 = ((f32[4,1024,32]{1,2,0:T(8,128)}), f32[4,1024,32]{1,2,0:T(8,128)S(1)}, u32[]{:S(2)}, u32[]{:S(2)}) async-start(f32[4,1024,32]{1,2,0:T(8,128)} %stack.81), calls=%async_computation.1 | async-start | bytes 1048576 | tf_op jit(solution)/shard_map/while/body/eval_jaxpr/all_to_all | solution.py:32
  62.2 14.8 %collective-permute-start = (f32[1024,32]{0,1:T(8,128)S(1)}, f32[1024,32]{0,1:T(8,128)S(1)}, u32[]{:S(2)}, u32[]{:S(2)}) collective-permute-start(f32[1024,32]{0,1:T(8,128)S(1)} %bitcast.117), channel_id=1, source_target_pairs={{0,4},{4,8},{8,12},{12,16},{16,20},{20,24},{24,28},{1,5},{5,9},{9,... | collective-permute-start | bytes 393224 | tf_op jit(solution)/shard_map/while/body/eval_jaxpr/ppermute | solution.py:12
  78.0 17.5 %all-to-all-start = ((f32[4,1024,32]{1,2,0:T(8,128)}), f32[4,1024,32]{1,2,0:T(8,128)S(1)}, u32[]{:S(2)}, u32[]{:S(2)}) async-start(f32[4,1024,32]{1,2,0:T(8,128)} %stack.80), calls=%async_computation | async-start | bytes 1048576 | tf_op jit(solution)/shard_map/while/body/eval_jaxpr/all_to_all | solution.py:32
  102.5 17.5 %all-to-all-start.1 = ((f32[4,1024,32]{1,2,0:T(8,128)}), f32[4,1024,32]{1,2,0:T(8,128)S(1)}, u32[]{:S(2)}, u32[]{:S(2)}) async-start(f32[4,1024,32]{1,2,0:T(8,128)} %stack.81), calls=%async_computation.1 | async-start | bytes 1048576 | tf_op jit(solution)/shard_map/while/body/eval_jaxpr/all_to_all | solution.py:32
  126.0 18.4 %collective-permute-start = (f32[1024,32]{0,1:T(8,128)S(1)}, f32[1024,32]{0,1:T(8,128)S(1)}, u32[]{:S(2)}, u32[]{:S(2)}) collective-permute-start(f32[1024,32]{0,1:T(8,128)S(1)} %bitcast.117), channel_id=1, source_target_pairs={{0,4},{4,8},{8,12},{12,16},{16,20},{20,24},{24,28},{1,5},{5,9},{9,... | collective-permute-start | bytes 393224 | tf_op jit(solution)/shard_map/while/body/eval_jaxpr/ppermute | solution.py:12
  145.4 16.9 %all-to-all-start = ((f32[4,1024,32]{1,2,0:T(8,128)}), f32[4,1024,32]{1,2,0:T(8,128)S(1)}, u32[]{:S(2)}, u32[]{:S(2)}) async-start(f32[4,1024,32]{1,2,0:T(8,128)} %stack.80), calls=%async_computation | async-start | bytes 1048576 | tf_op jit(solution)/shard_map/while/body/eval_jaxpr/all_to_all | solution.py:32
  169.2 18.3 %all-to-all-start.1 = ((f32[4,1024,32]{1,2,0:T(8,128)}), f32[4,1024,32]{1,2,0:T(8,128)S(1)}, u32[]{:S(2)}, u32[]{:S(2)}) async-start(f32[4,1024,32]{1,2,0:T(8,128)} %stack.81), calls=%async_computation.1 | async-start | bytes 1048576 | tf_op jit(solution)/shard_map/while/body/eval_jaxpr/all_to_all | solution.py:32
  193.6 16.9 %collective-permute-start = (f32[1024,32]{0,1:T(8,128)S(1)}, f32[1024,32]{0,1:T(8,128)S(1)}, u32[]{:S(2)}, u32[]{:S(2)}) collective-permute-start(f32[1024,32]{0,1:T(8,128)S(1)} %bitcast.117), channel_id=1, source_target_pairs={{0,4},{4,8},{8,12},{12,16},{16,20},{20,24},{24,28},{1,5},{5,9},{9,... | collective-permute-start | bytes 393224 | tf_op jit(solution)/shard_map/while/body/eval_jaxpr/ppermute | solution.py:12
  211.5 18.2 %all-to-all-start = ((f32[4,1024,32]{1,2,0:T(8,128)}), f32[4,1024,32]{1,2,0:T(8,128)S(1)}, u32[]{:S(2)}, u32[]{:S(2)}) async-start(f32[4,1024,32]{1,2,0:T(8,128)} %stack.80), calls=%async_computation | async-start | bytes 1048576 | tf_op jit(solution)/shard_map/while/body/eval_jaxpr/all_to_all | solution.py:32
  236.6 17.6 %all-to-all-start.1 = ((f32[4,1024,32]{1,2,0:T(8,128)}), f32[4,1024,32]{1,2,0:T(8,128)S(1)}, u32[]{:S(2)}, u32[]{:S(2)}) async-start(f32[4,1024,32]{1,2,0:T(8,128)} %stack.81), calls=%async_computation.1 | async-start | bytes 1048576 | tf_op jit(solution)/shard_map/while/body/eval_jaxpr/all_to_all | solution.py:32
  260.3 15.7 %collective-permute-start = (f32[1024,32]{0,1:T(8,128)S(1)}, f32[1024,32]{0,1:T(8,128)S(1)}, u32[]{:S(2)}, u32[]{:S(2)}) collective-permute-start(f32[1024,32]{0,1:T(8,128)S(1)} %bitcast.117), channel_id=1, source_target_pairs={{0,4},{4,8},{8,12},{12,16},{16,20},{20,24},{24,28},{1,5},{5,9},{9,... | collective-permute-start | bytes 393224 | tf_op jit(solution)/shard_map/while/body/eval_jaxpr/ppermute | solution.py:12
  277.1 17.5 %all-to-all-start = ((f32[4,1024,32]{1,2,0:T(8,128)}), f32[4,1024,32]{1,2,0:T(8,128)S(1)}, u32[]{:S(2)}, u32[]{:S(2)}) async-start(f32[4,1024,32]{1,2,0:T(8,128)} %stack.80), calls=%async_computation | async-start | bytes 1048576 | tf_op jit(solution)/shard_map/while/body/eval_jaxpr/all_to_all | solution.py:32
  301.5 17.5 %all-to-all-start.1 = ((f32[4,1024,32]{1,2,0:T(8,128)}), f32[4,1024,32]{1,2,0:T(8,128)S(1)}, u32[]{:S(2)}, u32[]{:S(2)}) async-start(f32[4,1024,32]{1,2,0:T(8,128)} %stack.81), calls=%async_computation.1 | async-start | bytes 1048576 | tf_op jit(solution)/shard_map/while/body/eval_jaxpr/all_to_all | solution.py:32
  325.1 15.8 %collective-permute-start = (f32[1024,32]{0,1:T(8,128)S(1)}, f32[1024,32]{0,1:T(8,128)S(1)}, u32[]{:S(2)}, u32[]{:S(2)}) collective-permute-start(f32[1024,32]{0,1:T(8,128)S(1)} %bitcast.117), channel_id=1, source_target_pairs={{0,4},{4,8},{8,12},{12,16},{16,20},{20,24},{24,28},{1,5},{5,9},{9,... | collective-permute-start | bytes 393224 | tf_op jit(solution)/shard_map/while/body/eval_jaxpr/ppermute | solution.py:12
  341.9 18.4 %all-to-all-start = ((f32[4,1024,32]{1,2,0:T(8,128)}), f32[4,1024,32]{1,2,0:T(8,128)S(1)}, u32[]{:S(2)}, u32[]{:S(2)}) async-start(f32[4,1024,32]{1,2,0:T(8,128)} %stack.80), calls=%async_computation | async-start | bytes 1048576 | tf_op jit(solution)/shard_map/while/body/eval_jaxpr/all_to_all | solution.py:32
  367.3 17.6 %all-to-all-start.1 = ((f32[4,1024,32]{1,2,0:T(8,128)}), f32[4,1024,32]{1,2,0:T(8,128)S(1)}, u32[]{:S(2)}, u32[]{:S(2)}) async-start(f32[4,1024,32]{1,2,0:T(8,128)} %stack.81), calls=%async_computation.1 | async-start | bytes 1048576 | tf_op jit(solution)/shard_map/while/body/eval_jaxpr/all_to_all | solution.py:32
  391.0 14.6 %collective-permute-start = (f32[1024,32]{0,1:T(8,128)S(1)}, f32[1024,32]{0,1:T(8,128)S(1)}, u32[]{:S(2)}, u32[]{:S(2)}) collective-permute-start(f32[1024,32]{0,1:T(8,128)S(1)} %bitcast.117), channel_id=1, source_target_pairs={{0,4},{4,8},{8,12},{12,16},{16,20},{20,24},{24,28},{1,5},{5,9},{9,... | collective-permute-start | bytes 393224 | tf_op jit(solution)/shard_map/while/body/eval_jaxpr/ppermute | solution.py:12
  406.6 17.5 %all-to-all-start = ((f32[4,1024,32]{1,2,0:T(8,128)}), f32[4,1024,32]{1,2,0:T(8,128)S(1)}, u32[]{:S(2)}, u32[]{:S(2)}) async-start(f32[4,1024,32]{1,2,0:T(8,128)} %stack.80), calls=%async_computation | async-start | bytes 1048576 | tf_op jit(solution)/shard_map/while/body/eval_jaxpr/all_to_all | solution.py:32
  431.1 17.5 %all-to-all-start.1 = ((f32[4,1024,32]{1,2,0:T(8,128)}), f32[4,1024,32]{1,2,0:T(8,128)S(1)}, u32[]{:S(2)}, u32[]{:S(2)}) async-start(f32[4,1024,32]{1,2,0:T(8,128)} %stack.81), calls=%async_computation.1 | async-start | bytes 1048576 | tf_op jit(solution)/shard_map/while/body/eval_jaxpr/all_to_all | solution.py:32
  454.6 14.6 %collective-permute-start = (f32[1024,32]{0,1:T(8,128)S(1)}, f32[1024,32]{0,1:T(8,128)S(1)}, u32[]{:S(2)}, u32[]{:S(2)}) collective-permute-start(f32[1024,32]{0,1:T(8,128)S(1)} %bitcast.117), channel_id=1, source_target_pairs={{0,4},{4,8},{8,12},{12,16},{16,20},{20,24},{24,28},{1,5},{5,9},{9,... | collective-permute-start | bytes 393224 | tf_op jit(solution)/shard_map/while/body/eval_jaxpr/ppermute | solution.py:12
  470.2 17.5 %all-to-all-start = ((f32[4,1024,32]{1,2,0:T(8,128)}), f32[4,1024,32]{1,2,0:T(8,128)S(1)}, u32[]{:S(2)}, u32[]{:S(2)}) async-start(f32[4,1024,32]{1,2,0:T(8,128)} %stack.80), calls=%async_computation | async-start | bytes 1048576 | tf_op jit(solution)/shard_map/while/body/eval_jaxpr/all_to_all | solution.py:32
  494.6 17.5 %all-to-all-start.1 = ((f32[4,1024,32]{1,2,0:T(8,128)}), f32[4,1024,32]{1,2,0:T(8,128)S(1)}, u32[]{:S(2)}, u32[]{:S(2)}) async-start(f32[4,1024,32]{1,2,0:T(8,128)} %stack.81), calls=%async_computation.1 | async-start | bytes 1048576 | tf_op jit(solution)/shard_map/while/body/eval_jaxpr/all_to_all | solution.py:32
  518.2 14.6 %collective-permute-start = (f32[1024,32]{0,1:T(8,128)S(1)}, f32[1024,32]{0,1:T(8,128)S(1)}, u32[]{:S(2)}, u32[]{:S(2)}) collective-permute-start(f32[1024,32]{0,1:T(8,128)S(1)} %bitcast.117), channel_id=1, source_target_pairs={{0,4},{4,8},{8,12},{12,16},{16,20},{20,24},{24,28},{1,5},{5,9},{9,... | collective-permute-start | bytes 393224 | tf_op jit(solution)/shard_map/while/body/eval_jaxpr/ppermute | solution.py:12
  533.9 17.5 %all-to-all-start = ((f32[4,1024,32]{1,2,0:T(8,128)}), f32[4,1024,32]{1,2,0:T(8,128)S(1)}, u32[]{:S(2)}, u32[]{:S(2)}) async-start(f32[4,1024,32]{1,2,0:T(8,128)} %stack.80), calls=%async_computation | async-start | bytes 1048576 | tf_op jit(solution)/shard_map/while/body/eval_jaxpr/all_to_all | solution.py:32
  558.3 17.5 %all-to-all-start.1 = ((f32[4,1024,32]{1,2,0:T(8,128)}), f32[4,1024,32]{1,2,0:T(8,128)S(1)}, u32[]{:S(2)}, u32[]{:S(2)}) async-start(f32[4,1024,32]{1,2,0:T(8,128)} %stack.81), calls=%async_computation.1 | async-start | bytes 1048576 | tf_op jit(solution)/shard_map/while/body/eval_jaxpr/all_to_all | solution.py:32
  581.9 14.6 %collective-permute-start = (f32[1024,32]{0,1:T(8,128)S(1)}, f32[1024,32]{0,1:T(8,128)S(1)}, u32[]{:S(2)}, u32[]{:S(2)}) collective-permute-start(f32[1024,32]{0,1:T(8,128)S(1)} %bitcast.117), channel_id=1, source_target_pairs={{0,4},{4,8},{8,12},{12,16},{16,20},{20,24},{24,28},{1,5},{5,9},{9,... | collective-permute-start | bytes 393224 | tf_op jit(solution)/shard_map/while/body/eval_jaxpr/ppermute | solution.py:12
  597.4 17.5 %all-to-all-start = ((f32[4,1024,32]{1,2,0:T(8,128)}), f32[4,1024,32]{1,2,0:T(8,128)S(1)}, u32[]{:S(2)}, u32[]{:S(2)}) async-start(f32[4,1024,32]{1,2,0:T(8,128)} %stack.80), calls=%async_computation | async-start | bytes 1048576 | tf_op jit(solution)/shard_map/while/body/eval_jaxpr/all_to_all | solution.py:32
  621.9 17.5 %all-to-all-start.1 = ((f32[4,1024,32]{1,2,0:T(8,128)}), f32[4,1024,32]{1,2,0:T(8,128)S(1)}, u32[]{:S(2)}, u32[]{:S(2)}) async-start(f32[4,1024,32]{1,2,0:T(8,128)} %stack.81), calls=%async_computation.1 | async-start | bytes 1048576 | tf_op jit(solution)/shard_map/while/body/eval_jaxpr/all_to_all | solution.py:32
  645.4 14.6 %collective-permute-start = (f32[1024,32]{0,1:T(8,128)S(1)}, f32[1024,32]{0,1:T(8,128)S(1)}, u32[]{:S(2)}, u32[]{:S(2)}) collective-permute-start(f32[1024,32]{0,1:T(8,128)S(1)} %bitcast.117), channel_id=1, source_target_pairs={{0,4},{4,8},{8,12},{12,16},{16,20},{20,24},{24,28},{1,5},{5,9},{9,... | collective-permute-start | bytes 393224 | tf_op jit(solution)/shard_map/while/body/eval_jaxpr/ppermute | solution.py:12
  661.0 17.5 %all-to-all-start = ((f32[4,1024,32]{1,2,0:T(8,128)}), f32[4,1024,32]{1,2,0:T(8,128)S(1)}, u32[]{:S(2)}, u32[]{:S(2)}) async-start(f32[4,1024,32]{1,2,0:T(8,128)} %stack.80), calls=%async_computation | async-start | bytes 1048576 | tf_op jit(solution)/shard_map/while/body/eval_jaxpr/all_to_all | solution.py:32
  685.4 17.5 %all-to-all-start.1 = ((f32[4,1024,32]{1,2,0:T(8,128)}), f32[4,1024,32]{1,2,0:T(8,128)S(1)}, u32[]{:S(2)}, u32[]{:S(2)}) async-start(f32[4,1024,32]{1,2,0:T(8,128)} %stack.81), calls=%async_computation.1 | async-start | bytes 1048576 | tf_op jit(solution)/shard_map/while/body/eval_jaxpr/all_to_all | solution.py:32
  (62 other events, 308.3 us)
